TPU v7x, 32 devices: a whole 2x2x4 slice. The times are simulated.
32 devices in a mesh: fsdp: 8 (over z, x), ctx: 2 (over y), tp: 2 (over core).
Axes of the slice: x: 2, y: 2, z: 4, core: 2. Of those that a mesh axis runs over, the one named last changes fastest.
Arguments:
- hidden_in: bfloat16 [4096, 2048], P(('fsdp', 'ctx', 'tp')), may hold values from -6 to 6
- cotangent: bfloat16 [4096, 2048], P(('fsdp', 'ctx', 'tp')), may hold values from -6 to 6
- segments: int32 [4096], P('fsdp'), may hold values from 0 to 31, never falling along the last dimension, each value on 1 to 512 neighbouring positions
- w_query: bfloat16 [2048, 2048], P(('fsdp', 'ctx'), 'tp'), may hold values from -0.125 to 0.125
- key_projection_weight: bfloat16 [2048, 1024], P(('fsdp', 'ctx'), 'tp'), may hold values from -0.125 to 0.125
- value_projection_weight: bfloat16 [2048, 1024], P(('fsdp', 'ctx'), 'tp'), may hold values from -0.125 to 0.125
- w_out: bfloat16 [2048, 2048], P('tp', ('fsdp', 'ctx')), may hold values from -0.5 to 0.5
- w_gate: bfloat16 [2048, 6144], P('fsdp', ('ctx', 'tp')), may hold values from -0.125 to 0.125
- w_up: bfloat16 [2048, 6144], P('fsdp', ('ctx', 'tp')), may hold values from -0.125 to 0.125
- w_down: bfloat16 [6144, 2048], P(('ctx', 'tp'), 'fsdp'), may hold values from -0.078125 to 0.078125
- gain_attn: float32 [2048], replicated, may hold values from 0.5 to 1.5
- gain_mlp: float32 [2048], replicated, may hold values from 0.5 to 1.5
- gain_query: float32 [128], replicated, may hold values from 0.6 to 1.6
- key_norm_gain: float32 [128], replicated, may hold values from 0.6 to 1.6
Outputs:
- hidden_out: float32 [4096, 2048], P(('fsdp', 'ctx', 'tp'))
- grad_input: float32 [4096, 2048], P(('fsdp', 'ctx', 'tp'))
- grad_w_query: float32 [2048, 2048], P(('fsdp', 'ctx'), 'tp')
- grad_w_key: float32 [2048, 1024], P(('fsdp', 'ctx'), 'tp')
- grad_w_value: float32 [2048, 1024], P(('fsdp', 'ctx'), 'tp')
- grad_w_out: float32 [2048, 2048], P('tp', ('fsdp', 'ctx'))
- grad_w_gate: float32 [2048, 6144], P('fsdp', ('ctx', 'tp'))
- grad_w_up: float32 [2048, 6144], P('fsdp', ('ctx', 'tp'))
- grad_w_down: float32 [6144, 2048], P(('ctx', 'tp'), 'fsdp')
- grad_gain_attn: float32 [2048], replicated
- grad_gain_mlp: float32 [2048], replicated
- grad_gain_query: float32 [128], replicated
- grad_gain_key: float32 [128], replicated
Inputs may be any that keep to these rules, and one draw needn't show every extreme that they name: `segments`: segment numbers never fall along the tokens, and every number up to the largest names a run of 1 to 512 tokens.
All inputs are finite; a program needn't handle non-finite values.
Results may differ from a plain program's by a relative error of at most 0.014.
Values may be sent and summed in bfloat16 or wider, within the bound.
A program may use at most 256 MiB of HBM per device.

v0:
```python
import functools

import jax
import jax.numpy as jnp
from jax import lax
from jax.experimental import pallas as pl
from jax.experimental.pallas import tpu as pltpu
from jax.sharding import PartitionSpec as P

EPS = 1e-06
THETA = 1000000.0
AXES = ("fsdp", "ctx", "tp")
MESH = pl.DeviceIdType.MESH
BF16 = jnp.bfloat16
F32 = jnp.float32
TP_BIT, CTX_BIT = 1, 2
PAIR = 2
PAIR_BIT = PAIR * 4


def dot_rows(left, right):
    return lax.dot_general(left, right, (((0,), (0,)), ((), ())), preferred_element_type=F32)


def dot_cols(left, right):
    return lax.dot_general(left, right, (((1,), (1,)), ((), ())), preferred_element_type=F32)


def dot(left, right):
    return lax.dot_general(left, right, (((1,), (0,)), ((), ())), preferred_element_type=F32)


def remote(src, dst, send, recv, device):
    return pltpu.make_async_remote_copy(
        src_ref=src, dst_ref=dst, send_sem=send, recv_sem=recv, device_id=device, device_id_type=MESH
    )


class Moves:
    def __init__(self, send, recv, local):
        self.send, self.recv, self.local = send, recv, local
        self.sent, self.loads = 0, 0
        self.open = []

    def swap(self, src, there, here, device, open_=None):
        k = self.sent
        self.sent += 1
        copy = remote(src, there, self.send.at[k], self.recv.at[k], device)
        copy.start()
        (self.open if open_ is None else open_).append(copy.wait_send)
        return remote(src, here, self.send.at[k], self.recv.at[k], device).wait_recv

    def load(self, src, dst):
        k = self.loads
        self.loads += 1
        copy = pltpu.make_async_copy(src, dst, self.local.at[k])
        copy.start()
        return copy.wait

    def store(self, src, dst):
        self.open.append(self.load(src, dst))

    def close(self):
        for wait in self.open:
            wait()


class Place:
    def __init__(self, bits):
        self.bits = bits
        f, c, t = lax.axis_index("fsdp"), lax.axis_index("ctx"), lax.axis_index("tp")
        self.f, self.c, self.t = f, c, t
        self.pair = (f // PAIR) % 2
        far_f = self.block(PAIR)
        fs, cs = [f, f, far_f, far_f], [c, 1 - c, c, 1 - c]
        pairs = [self.pair, self.pair, 1 - self.pair, 1 - self.pair]
        self.at = [(fs[j], cs[j], pairs[j]) for j in range(4)]
        self.rows_of = [pairs[j] * 4 + cs[j] * 2 for j in range(4)]
        self.chunk_of = [cs[j] * 2 + pairs[j] for j in range(4)]
        self.relay = len(bits) == 2
        self.across_mask = bits[0] | PAIR
        self.inner = (f // bits[0]) % 2 != self.pair
        self.chips = [None, {"ctx": 1 - c}, {"fsdp": far_f}, {"fsdp": far_f, "ctx": 1 - c}]
        self.sibling = {"tp": 1 - t}

    def block(self, mask):
        out = self.f
        for i in range(mask.bit_length()):
            b = 1 << i
            if mask & b:
                out = out + b - 2 * b * ((self.f // b) % 2)
        return out

    def along(self, bit):
        return {"fsdp": self.block(bit)}

    def greet(self):
        barrier = pltpu.get_barrier_semaphore()
        devices = [*self.chips[1:], self.sibling, *[self.along(b) for b in self.bits]]
        if self.relay:
            devices += [self.along(self.across_mask), self.along(self.bits[0] | self.bits[1])]
        for device in devices:
            pl.semaphore_signal(barrier, inc=1, device_id=device, device_id_type=MESH)
        pl.semaphore_wait(barrier, len(devices))


class Cross:
    def __init__(self, moves, place, src, here, came_in, across_to, came_out, pair_to):
        self.place, self.here = place, here
        self.came_in, self.came_out = came_in, came_out
        k = moves.sent
        moves.sent += 4
        pair, across = place.chips[2], place.along(place.across_mask)

        def copy(i, source, to, device):
            return remote(source, to, moves.send.at[k + i], moves.recv.at[k + i], device)

        self.hand = copy(0, src, came_in, pair)
        self.own = copy(1, src, came_out, across)
        self.on = copy(2, came_in, across_to, across)
        self.back = copy(3, came_out, pair_to, pair)
        self.came = [copy(0, came_in, came_in, pair), copy(1, came_out, came_out, across)]
        self.landed = [copy(2, here, here, across), copy(3, here, here, pair)]
        moves.open.append(self.left)

        @pl.when(place.inner)
        def _():
            self.own.start()

        @pl.when(jnp.logical_not(place.inner))
        def _():
            self.hand.start()

    def relay(self):
        @pl.when(self.place.inner)
        def _():
            self.came[0].wait_recv()
            self.on.start()
            self.came[1].wait_recv()
            self.back.start()

    def arrive(self):
        @pl.when(self.place.inner)
        def _():
            self.landed[0].wait_recv()

        @pl.when(jnp.logical_not(self.place.inner))
        def _():
            self.landed[1].wait_recv()

    def left(self):
        @pl.when(self.place.inner)
        def _():
            self.own.wait_send()
            self.on.wait_send()
            self.back.wait_send()

        @pl.when(jnp.logical_not(self.place.inner))
        def _():
            self.hand.wait_send()


class Spread:
    def __init__(self, moves, place, own, out, part=0, parts=1):
        self.moves, self.place, self.out = moves, place, out
        self.rows = own.shape[0]
        self.stride, self.offset = self.rows * parts, self.rows * part
        self.open = []
        mine = self.at(0, place.t)
        self.here = moves.load(own, mine)
        self.pair = moves.swap(own, mine, self.at(2, place.t), place.chips[2], self.open)
        self.ctx = moves.swap(own, mine, self.at(1, place.t), place.chips[1], self.open)
        self.beside = [moves.swap(own, mine, self.at(0, 1 - place.t), place.sibling, self.open)]

    def at(self, j, t):
        start = (self.place.rows_of[j] + t) * self.stride + self.offset
        return self.out.at[pl.ds(pl.multiple_of(start, self.rows), self.rows)]

    def hand(self, j):
        block = self.at(j, self.place.t)
        self.beside.append(
            self.moves.swap(block, block, self.at(j, 1 - self.place.t), self.place.sibling, self.open)
        )

    def from_pair(self):
        self.pair()
        block = self.at(2, self.place.t)
        self.both = self.moves.swap(block, block, self.at(3, self.place.t), self.place.chips[1], self.open)
        self.hand(2)

    def from_ctx(self):
        self.ctx()
        self.hand(1)

    def from_both(self):
        self.both()
        self.hand(3)

    def finish(self):
        self.here()
        for wait in (*self.beside, *self.open):
            wait()


class Collect:
    def __init__(self, moves, place, part, held, first, ctx_in, pair_in, sending, load):
        self.moves, self.place = moves, place
        self.first, self.ctx_in, self.pair_in, self.sending = first, ctx_in, pair_in, sending
        t = place.t
        self.hands, self.loads, self.open = {}, {}, []
        for j in (3, 1, 2, 0):
            self.hands[j] = moves.swap(part(j, 1 - t), first.at[j], first.at[j], place.sibling, self.open)
            if load:
                self.loads[j] = moves.load(part(j, t), held.at[j])
        self.held = (lambda j: held.at[j]) if load else (lambda j: part(j, t))

    def two(self, j, at):
        return self.held(j)[at].astype(F32) + self.first[j, at].astype(F32)

    def ready(self, j):
        self.hands[j]()
        if j in self.loads:
            self.loads[j]()

    def to_ctx(self):
        self.waits = {}
        for j, slot in ((3, 0), (1, 1)):
            self.ready(j)

            def body(at):
                self.sending[slot, at] = self.two(j, at).astype(BF16)

            row_loop(self.sending.shape[1], body)
            self.waits[j] = self.moves.swap(
                self.sending.at[slot], self.ctx_in.at[slot], self.ctx_in.at[slot], self.place.chips[1], self.open
            )

    def to_pair(self):
        self.ready(2)
        self.waits[3]()

        def body(at):
            self.sending[2, at] = (self.two(2, at) + self.ctx_in[0, at].astype(F32)).astype(BF16)

        row_loop(self.sending.shape[1], body)
        self.waits[2] = self.moves.swap(
            self.sending.at[2], self.pair_in, self.pair_in, self.place.chips[2], self.open
        )

    def fold(self):
        for j, slot in ((3, 0), (1, 1), (2, 2)):
            self.ready(j)

            def body(at):
                self.sending[slot, at] = self.two(j, at).astype(BF16)

            row_loop(self.sending.shape[1], body)
        self.ready(0)

    def post_ctx(self):
        self.waits = {}
        for j, slot in ((3, 0), (1, 1)):
            self.waits[j] = self.moves.swap(
                self.sending.at[slot], self.ctx_in.at[slot], self.ctx_in.at[slot], self.place.chips[1], self.open
            )

    def post_pair(self):
        self.waits[3]()

        def body(at):
            self.sending[2, at] = (self.sending[2, at].astype(F32) + self.ctx_in[0, at].astype(F32)).astype(BF16)

        row_loop(self.sending.shape[1], body)
        self.waits[2] = self.moves.swap(
            self.sending.at[2], self.pair_in, self.pair_in, self.place.chips[2], self.open
        )

    def came(self):
        for wait in (self.waits[1], self.waits[2], *self.open):
            wait()

    def finish(self):
        self.ready(0)
        self.waits[1]()
        self.waits[2]()
        for wait in self.open:
            wait()

    def total(self, at):
        return self.two(0, at) + (self.ctx_in[1, at].astype(F32) + self.pair_in[at].astype(F32))


def collect_buffers(rows, width):
    return [
        pltpu.VMEM((4, rows, width), BF16),
        pltpu.VMEM((2, rows, width), BF16),
        pltpu.VMEM((rows, width), BF16),
        pltpu.VMEM((3, rows, width), BF16),
    ]


def row_loop(rows, body):
    step = 16

    @pl.loop(0, rows // step)
    def _(i):
        body(pl.ds(pl.multiple_of(i * step, step), step))


def half_loop(part, rows, body):
    step = 16

    @pl.loop(0, rows // step)
    def _(i):
        body(
            pl.ds(pl.multiple_of(i * step, step), step),
            pl.ds(pl.multiple_of(part * rows + i * step, step), step),
        )


def unit_and_scale(x):
    scale = lax.rsqrt(jnp.mean(x * x, axis=-1, keepdims=True) + EPS)
    return x * scale, scale


class Gather:
    def __init__(self, moves, place, block, spare):
        self.moves, self.place, self.block, self.spare = moves, place, block, spare
        self.waits, self.crosses = {}, {}

    def forward(self, mask, src=None):
        done = [i for i, b in enumerate(self.place.bits) if mask & b]
        here = self.block(self.place.block(mask))
        for b in self.place.bits[max(done, default=-1) + 1 :]:
            if self.place.relay and b == self.place.bits[0]:
                far = self.place.across_mask
                slot = 0 if mask == 0 else 2
                self.crosses[mask] = Cross(
                    self.moves, self.place, here if src is None else src, self.block(self.place.block(mask | b)),
                    self.spare.at[slot], self.block(self.place.block(mask ^ PAIR)),
                    self.spare.at[slot + 1], self.block(self.place.block(mask ^ far)),
                )
                self.waits[mask | b] = self.crosses[mask].arrive
                continue
            self.waits[mask | b] = self.moves.swap(
                here if src is None else src, here, self.block(self.place.block(mask | b)), self.place.along(b)
            )

    def masks(self, stage):
        out = [0, PAIR]
        for b in self.place.bits[:stage]:
            out += [m | b for m in out]
        return [m | self.place.bits[stage] for m in out]

    def relay(self, m):
        if self.place.relay:
            self.crosses[m].relay()

    def hop(self, m):
        if self.place.relay:
            self.pass_on(m | self.place.bits[0])
        elif m == PAIR:
            self.middle()

    def pass_on(self, m):
        self.waits.pop(m)()
        self.forward(m)

    def middle(self):
        for stage in range(len(self.place.bits) - 1):
            for m in self.masks(stage):
                if m in self.waits:
                    self.pass_on(m)

    def finish(self):
        for wait in self.waits.values():
            wait()


def head_unit(x):
    scale = lax.rsqrt(jnp.mean(x * x, axis=-1, keepdims=True) + EPS)
    return x * scale, scale


def rot(a, cos, sin):
    return a * cos + pltpu.roll(a, a.shape[-1] // 2, 1) * sin


def rot_back(b, cos, sin):
    return b * cos - pltpu.roll(b, b.shape[-1] // 2, 1) * sin


def allowed_keys(start):
    length = start.shape[0]
    row = lax.broadcasted_iota(jnp.int32, (length, length), 0)
    col = lax.broadcasted_iota(jnp.int32, (length, length), 1)
    return (col.astype(F32) >= start) & (row >= col)


def soft_of(scores):
    peak = jnp.max(scores, axis=-1, keepdims=True)
    lse = peak + jnp.log(jnp.sum(jnp.exp(scores - peak), axis=-1, keepdims=True))
    return jnp.exp(scores - lse)


def attend_one(groups, s, qkv, starts, cos_ref, sin_ref, gain_q, gain_k, out):
    d = gain_q.shape[-1]
    length = cos_ref.shape[0] // 2
    rows = pl.ds(pl.multiple_of(s * length, length), length)
    cos, sin = cos_ref[rows], sin_ref[rows]
    allowed = allowed_keys(starts[rows, 0:1])
    unit_k, _ = head_unit(qkv[rows, groups * d : (groups + 1) * d].astype(F32))
    key = rot(unit_k * gain_k[...], cos, sin).astype(BF16)
    value = qkv[rows, (groups + 1) * d : (groups + 2) * d]
    for g in range(groups):
        unit_q, _ = head_unit(qkv[rows, g * d : (g + 1) * d].astype(F32))
        query = rot(unit_q * gain_q[...], cos, sin).astype(BF16)
        scores = jnp.where(allowed, dot_cols(query, key) * d**-0.5, -jnp.inf)
        soft = soft_of(scores).astype(BF16)
        out[rows, g * d : (g + 1) * d] = dot(soft, value).astype(BF16)


def through_norm(b, unit, scale, gain):
    e = b * gain
    return scale * (e - unit * jnp.mean(e * unit, axis=-1, keepdims=True))


def attend_back_one(
    groups, s, qkv, att, datt, starts, cos_ref, sin_ref, gain_q, gain_k, grad, gains
):
    d = gain_q.shape[-1]
    length = cos_ref.shape[0] // 2
    rows = pl.ds(pl.multiple_of(s * length, length), length)
    cos, sin = cos_ref[rows], sin_ref[rows]
    scale = d**-0.5
    allowed = allowed_keys(starts[rows, 0:1])
    at_k, at_v = slice(groups * d, (groups + 1) * d), slice((groups + 1) * d, (groups + 2) * d)
    unit_k, scale_k = head_unit(qkv[rows, at_k].astype(F32))
    key = rot(unit_k * gain_k[...], cos, sin).astype(BF16)
    value = qkv[rows, at_v]
    key_grad = jnp.zeros(unit_k.shape, F32)
    value_grad = jnp.zeros(unit_k.shape, F32)
    for g in range(groups):
        at = slice(g * d, (g + 1) * d)
        unit_q, scale_q = head_unit(qkv[rows, at].astype(F32))
        query = rot(unit_q * gain_q[...], cos, sin).astype(BF16)
        scores = jnp.where(allowed, dot_cols(query, key) * scale, -jnp.inf)
        soft = soft_of(scores)
        up = datt[rows, at]
        delta = jnp.sum(up.astype(F32) * att[rows, at].astype(F32), axis=-1, keepdims=True)
        ds = (soft * (dot_cols(up, value) - delta) * scale).astype(BF16)
        value_grad += dot_rows(soft.astype(BF16), up)
        key_grad += dot_rows(ds, query)
        b = rot_back(dot(ds, key), cos, sin)
        gains[0] += jnp.sum((b * unit_q).reshape(-1, 8, d), axis=0)
        grad[rows, at] = through_norm(b, unit_q, scale_q, gain_q[...]).astype(BF16)
    b = rot_back(key_grad, cos, sin)
    gains[1] += jnp.sum((b * unit_k).reshape(-1, 8, d), axis=0)
    grad[rows, at_k] = through_norm(b, unit_k, scale_k, gain_k[...]).astype(BF16)
    grad[rows, at_v] = value_grad.astype(BF16)


def attend_back_kernel(
    groups, qkv, att, datt, starts, cos, sin, gain_q, gain_k, grad, gains
):
    gains[...] = jnp.zeros_like(gains)

    @pl.loop(0, 2)
    def _(s):
        attend_back_one(groups, s, qkv, att, datt, starts, cos, sin, gain_q, gain_k, grad, gains)


def attend_back(groups, qkv, att, datt, common):
    n_rows, width = qkv.shape
    d = width // (groups + 2)
    length = n_rows // 2
    return pl.pallas_call(
        functools.partial(attend_back_kernel, groups),
        out_shape=(jax.ShapeDtypeStruct(qkv.shape, BF16), jax.ShapeDtypeStruct((2, 8, d), F32)),
        compiler_params=pltpu.CompilerParams(vmem_limit_bytes=40 << 20),
        cost_estimate=pl.CostEstimate(
            flops=n_rows * groups * length * (10 * d + 30),
            bytes_accessed=n_rows * width * 8,
            transcendentals=n_rows * groups * length * 2,
        ),
        name="attend_back",
    )(qkv, att, datt, *common)


def forward_kernel(
    bits, groups, natural,
    hidden, cot, gain_attn, gain_mlp, seg, table, gain_q, gain_k, wq, wk, wv, wo, wg, wu, wd,
    mid, normed_one, normed_two, cot_out, qkv_out, att_out, qkv_weight, out_weight, starts_out, cos_out, sin_out,
    grad_gate_out, grad_up_out, mixed_out, part_out, down_out, spare_qkv, spare_out,
    spare_gate_a, spare_up_a, spare_down_a, spare_gate_b, spare_up_b, spare_down_b, early_in,
    own_one, own_two, rows_one, rows_two, rows_cot, w_qkv, w_out, w_gate, w_up, w_down, qkv, att, part,
    gate, up, grad_gate, grad_up, mixed, mixed_t, starts, cos, sin, seg_in, early, first, ctx_in, pair_in, sending,
    send, recv, local,
):
    place = Place(bits)
    moves = Moves(send, recv, local)
    rows, width = hidden.shape
    at_rows, ff_rows, ff_cols = wq.shape[0], wg.shape[0], wg.shape[1] // 2
    q_cols, kv_cols = wq.shape[1] // 4, wk.shape[1] // 4
    n_rows, length = rows_one.shape[0], seg.shape[1]

    def lanes(start, size):
        return pl.ds(pl.multiple_of(start, size), size)

    def qkv_rows(f, c=None):
        if c is None:
            return lanes(f * 2 * at_rows, 2 * at_rows)
        return lanes((f * 2 + c) * at_rows, at_rows)

    place.greet()

    def out_block(f, c=None):
        return w_out.at[:, qkv_rows(f, c)] if natural else w_out.at[qkv_rows(f, c)]

    def out_chunk(j):
        at = lanes(place.chunk_of[j] * q_cols, q_cols)
        return wo.at[at] if natural else wo.at[:, at]

    pieces = (
        (wq, q_cols, pl.ds(0, q_cols)),
        (wk, kv_cols, pl.ds(q_cols, kv_cols)),
        (wv, kv_cols, pl.ds(q_cols + kv_cols, kv_cols)),
    )
    f0, c0, _ = place.at[0]
    qkv_in, out_in = {}, {}

    border = ff_cols - 256 if ff_cols % 256 == 0 and ff_cols > 256 else ff_cols // 2
    piece_a, piece_b = pl.ds(0, border), pl.ds(border, ff_cols - border)

    def feed_weight(weight, piece, source, spare, by_rows):
        start, size = (0, border) if piece is piece_a else (border, ff_cols - border)

        def block(f):
            at = lanes(f * ff_rows, ff_rows)
            return weight.at[at, piece] if by_rows else weight.at[piece, at]

        def half(which):
            at = pl.ds(pl.multiple_of(which * ff_cols + start, 128), size)
            return source.at[:, at] if by_rows else source.at[at]

        return Gather(moves, place, block, spare), half(place.pair), half(1 - place.pair)

    feed = []
    for piece, spares in ((piece_a, (spare_gate_a, spare_up_a, spare_down_a)), (piece_b, (spare_gate_b, spare_up_b, spare_down_b))):
        feed.append(feed_weight(w_gate, piece, wg, spares[0], True))
        feed.append(feed_weight(w_up, piece, wu, spares[1], True))
        feed.append(feed_weight(w_down, piece, wd, spares[2], not natural))
    own_feed = [moves.load(own, gather.block(place.f)) for gather, own, _ in feed]

    def swap_pair(i):
        gather, _, other = feed[i]
        gather.waits[PAIR] = moves.swap(
            other, gather.block(place.f), gather.block(place.block(PAIR)), place.along(PAIR)
        )

    early_waits = []

    def send_early(i):
        if place.relay:
            high, low = bits
            mask = (high, high | PAIR)[i] | low
            at = lanes(place.block(mask) * ff_rows, ff_rows)
            early[i] = dot(mixed_t[...], rows_cot[:, at]).astype(BF16)
            early_waits.append(moves.swap(early.at[i], early_in.at[i], early_in.at[i], place.along(low)))

    step = 2 * rows
    wide = min(256, w_qkv.shape[1])
    qkv_gather = Gather(moves, place, lambda f: w_qkv.at[qkv_rows(f)], spare_qkv)
    out_gather = Gather(moves, place, out_block, spare_out)

    def norm_one(at):
        unit, _ = unit_and_scale(hidden[at].astype(F32))
        own_one[at] = (unit * gain_attn[...]).astype(BF16)

    collects = [None, None]

    def collect_part(h):
        at = pl.ds(h * rows // 2, rows // 2)
        return Collect(
            moves, place, lambda j, t: part.at[place.rows_of[j] + t, at], None, first.at[:, at], ctx_in.at[:, at],
            pair_in.at[at], sending.at[:, at], False,
        )

    def norm_two(h):
        def body(there, at):
            x = hidden[at].astype(F32) + collects[h].total(there)
            mid[at] = x
            unit, _ = unit_and_scale(x)
            own_two[at] = (unit * gain_mlp[...]).astype(BF16)

        return body

    def columns_of(weight, at):
        return (dot, weight[:, at]) if natural else (dot_cols, weight[at])

    def gate_part(piece):
        @pl.loop(0, n_rows // step)
        def _(i):
            at = lanes(i * step, step)
            gate[at, piece] = dot(rows_two[at], w_gate[:, piece])

    def up_part(piece):
        @pl.loop(0, n_rows // step)
        def _(i):
            at = lanes(i * step, step)
            u = dot(rows_two[at], w_up[:, piece])
            up[at, piece] = u
            g = gate[at, piece]
            mix = g * jax.nn.sigmoid(g) * u
            mixed[at, piece] = mix.astype(BF16)
            mixed_t[piece, at] = mix.T.astype(BF16)

    def back_part(piece):
        @pl.loop(0, n_rows // step)
        def _(i):
            at = lanes(i * step, step)
            m = dot_cols(rows_cot[at], w_down[piece]) if natural else dot(rows_cot[at], w_down[:, piece])
            g = gate[at, piece]
            s = jax.nn.sigmoid(g)
            grad_gate[at, piece] = (m * up[at, piece] * s * (1.0 + g * (1.0 - s))).astype(BF16)
            grad_up[at, piece] = (m * (g * s)).astype(BF16)

    def grad_part(piece, last):
        for half in range(2):

            @pl.loop(0, width // 512)
            def _(i):
                at = lanes(half * (width // 2) + i * 256, 256)
                both = dot_cols(grad_gate[:, piece], w_gate[at, piece]) + dot_cols(grad_up[:, piece], w_up[at, piece])
                both = both.reshape(8, rows, 256)
                if last:
                    both = both + part[:, :, at].astype(F32)
                part[:, :, at] = both.astype(BF16)

            if last:
                at = pl.ds(half * (width // 2), width // 2)
                moves.store(part.at[:, :, at], part_out.at[:, :, at])

    def down_part(piece, last):
        @pl.loop(0, width // 256)
        def _(i):
            at = lanes(i * 256, 256)
            if natural:
                term = dot(mixed[:, piece], w_down[piece, at])
            else:
                term = dot_cols(mixed[:, piece], w_down[at, piece])
            if last:
                term = term + rows_one[:, at].astype(F32)
            rows_one[:, at] = term.astype(BF16)

        if last:
            moves.store(rows_one, down_out)

    for j in (3, 2, 1):
        fj, cj, _ = place.at[j]
        out_in[j] = moves.swap(out_chunk(j), out_block(f0, c0), out_block(fj, cj), place.chips[j])
    out_in[0] = moves.load(out_chunk(0), out_block(f0, c0))
    for j in (1, 3, 2):
        fj, cj, _ = place.at[j]
        qkv_in[j] = [
            moves.swap(
                w.at[:, lanes(place.chunk_of[j] * size, size)],
                w_qkv.at[qkv_rows(f0, c0), to],
                w_qkv.at[qkv_rows(fj, cj), to],
                place.chips[j],
            )
            for w, size, to in pieces
        ]
    qkv_in[0] = [
        moves.load(w.at[:, lanes(place.chunk_of[0] * size, size)], w_qkv.at[qkv_rows(f0, c0), to])
        for w, size, to in pieces
    ]
    out_in[0]()
    out_in[1]()
    out_gather.forward(0)
    for wait in (*qkv_in[0], *qkv_in[1]):
        wait()
    qkv_gather.forward(0)
    for wait in (*qkv_in[2], *qkv_in[3]):
        wait()
    qkv_gather.forward(PAIR)
    out_in[2]()
    out_in[3]()
    out_gather.forward(PAIR)
    row_loop(rows, norm_one)
    spread_one = Spread(moves, place, own_one, rows_one)
    out_gather.relay(0)
    seg_wait = moves.swap(seg, seg_in, seg_in, place.chips[2])
    qkv_gather.relay(0)
    swap_pair(1)
    qkv_gather.relay(PAIR)
    feed[2][0].forward(0, feed[2][1])
    swap_pair(2)
    qkv_gather.hop(0)
    out_gather.relay(PAIR)
    feed[3][0].forward(0, feed[3][1])
    out_gather.hop(0)
    spread_one.from_pair()
    qkv_gather.hop(PAIR)
    feed[0][0].forward(0, feed[0][1])
    spread_cot = Spread(moves, place, cot, rows_cot)
    spread_one.from_both()
    out_gather.hop(PAIR)
    spread_one.from_ctx()
    feed[1][0].forward(0, feed[1][1])
    seg_wait()
    pair_first = place.pair == 0
    own_seg, far_seg = seg[...].astype(F32), seg_in[...].astype(F32)
    for i in range(2):
        here = pair_first if i == 0 else jnp.logical_not(pair_first)
        flags = jnp.where(here, own_seg, far_seg)
        both = jnp.broadcast_to(flags, (128, length)).T[:, 0:1]
        start = jnp.sum((flags < both).astype(F32), axis=1, keepdims=True)
        row = lax.broadcasted_iota(jnp.int32, (length, length), 0).astype(F32)
        col = lax.broadcasted_iota(jnp.int32, (length, length), 1).astype(F32)
        chosen = (row - start == col).astype(F32)
        at = pl.ds(i * length, length)
        both_tables = lax.dot_general(
            chosen, table[...], (((1,), (0,)), ((), ())),
            precision=lax.Precision.HIGHEST, preferred_element_type=F32,
        )
        d = gain_q.shape[1]
        starts[at] = jnp.broadcast_to(start, (length, 128))
        cos[at] = both_tables[:, :d]
        sin[at] = both_tables[:, d:]
    moves.store(starts, starts_out)
    moves.store(cos, cos_out)
    moves.store(sin, sin_out)
    feed[2][0].pass_on(PAIR)
    spread_one.finish()
    normed_stored = moves.load(rows_one, normed_one)
    feed[2][0].relay(0)
    feed[1][0].pass_on(PAIR)
    swap_pair(0)
    qkv_gather.finish()
    moves.store(w_qkv, qkv_weight)
    swap_pair(3)
    feed[0][0].relay(0)
    @pl.loop(0, w_qkv.shape[1] // wide)
    def _(i):
        at = lanes(i * wide, wide)
        qkv[:, at] = dot(rows_one[...], w_qkv[:, at]).astype(BF16)

    moves.store(qkv, qkv_out)
    @pl.loop(0, 2)
    def _(s):
        attend_one(groups, s, qkv, starts, cos, sin, gain_q, gain_k, att)

    moves.store(att, att_out)
    swap_pair(4)
    out_gather.finish()
    moves.store(w_out, out_weight)
    feed[2][0].hop(0)
    feed[4][0].forward(0, feed[4][1])
    @pl.loop(0, width // 256)
    def _(i):
        at = lanes(i * 256, 256)
        times, block = columns_of(w_out, at)
        part[:, :, at] = times(att[...], block).astype(BF16).reshape(8, rows, 256)

    collects[0] = collect_part(0)
    feed[1][0].relay(0)
    collects[0].to_ctx()
    collects[1] = collect_part(1)
    feed[3][0].relay(0)
    feed[1][0].relay(PAIR)
    feed[1][0].hop(0)
    collects[1].to_ctx()
    feed[2][0].relay(PAIR)
    feed[0][0].pass_on(PAIR)
    spread_cot.from_pair()
    collects[1].to_pair()
    spread_cot.from_ctx()
    collects[0].to_pair()
    feed[3][0].pass_on(PAIR)
    feed[2][0].hop(PAIR)
    feed[0][0].relay(PAIR)
    feed[3][0].hop(0)
    feed[0][0].hop(0)
    collects[1].finish()
    half_loop(1, rows // 2, norm_two(1))
    spread_two_1 = Spread(moves, place, own_two.at[pl.ds(1 * rows // 2, rows // 2)], rows_two, 1, 2)
    feed[1][0].hop(PAIR)
    own_feed[2]()
    feed[2][0].finish()
    collects[0].finish()
    half_loop(0, rows // 2, norm_two(0))
    spread_two_0 = Spread(moves, place, own_two.at[pl.ds(0 * rows // 2, rows // 2)], rows_two, 0, 2)
    feed[0][0].hop(PAIR)
    spread_cot.from_both()
    feed[4][0].pass_on(PAIR)
    feed[3][0].relay(PAIR)
    spread_two_1.from_pair()
    swap_pair(5)
    feed[4][0].relay(0)
    spread_cot.finish()
    moves.store(rows_cot, cot_out)
    own_feed[0]()
    feed[0][0].finish()
    spread_two_0.from_pair()
    feed[3][0].hop(PAIR)
    spread_two_0.from_ctx()
    spread_two_1.from_ctx()
    feed[5][0].forward(0, feed[5][1])
    feed[4][0].relay(PAIR)
    spread_two_1.from_both()
    own_feed[3]()
    feed[3][0].finish()
    own_feed[1]()
    feed[1][0].finish()
    feed[4][0].hop(0)
    feed[5][0].pass_on(PAIR)
    spread_two_0.from_both()
    spread_two_1.finish()
    feed[4][0].hop(PAIR)
    feed[5][0].relay(0)
    spread_two_0.finish()
    moves.store(rows_two, normed_two)
    gate_part(piece_a)
    feed[5][0].relay(PAIR)
    gate_part(piece_b)
    up_part(piece_a)
    feed[5][0].hop(0)
    own_feed[4]()
    feed[4][0].finish()
    feed[5][0].hop(PAIR)
    up_part(piece_b)
    send_early(0)
    send_early(1)
    normed_stored()
    down_part(piece_a, False)
    own_feed[5]()
    feed[5][0].finish()
    back_part(piece_a)
    back_part(piece_b)
    down_part(piece_b, True)
    grad_part(piece_a, False)
    grad_part(piece_b, True)
    moves.store(mixed_t, mixed_out)
    moves.store(grad_gate, grad_gate_out)
    moves.store(grad_up, grad_up_out)
    for wait in early_waits:
        wait()
    moves.close()


def norm_back(grad, x, gain, gain_grad):
    unit, scale = unit_and_scale(x)
    gain_grad[...] += jnp.sum((grad * unit).reshape(-1, 8, grad.shape[-1]), axis=0)
    e = grad * gain
    return scale * (e - unit * jnp.mean(e * unit, axis=-1, keepdims=True))


def turn_kernel(
    bits, partial, mid, cot, gain, grad_mid, gain_grad, out,
    own, held, first, ctx_in, pair_in, sending, send, recv, local,
):
    place = Place(bits)
    moves = Moves(send, recv, local)
    place.greet()
    collect = Collect(
        moves, place, lambda j, t: partial.at[place.rows_of[j] + t], held, first, ctx_in, pair_in, sending, True
    )
    collect.to_ctx()
    collect.to_pair()
    collect.finish()
    gain_grad[...] = jnp.zeros_like(gain_grad)

    def back(at):
        g = cot[at].astype(F32) + norm_back(collect.total(at), mid[at], gain[...], gain_grad)
        grad_mid[at] = g
        own[at] = g.astype(BF16)

    row_loop(mid.shape[0], back)
    spread = Spread(moves, place, own, out)
    spread.from_pair()
    spread.from_ctx()
    spread.from_both()
    spread.finish()
    moves.close()


def last_kernel(
    bits, partial, hidden, grad_mid, gain, grad_in, gain_grad,
    held, first, ctx_in, pair_in, sending, send, recv, local,
):
    place = Place(bits)
    moves = Moves(send, recv, local)
    place.greet()
    collect = Collect(
        moves, place, lambda j, t: partial.at[place.rows_of[j] + t], held, first, ctx_in, pair_in, sending, True
    )
    collect.to_ctx()
    collect.to_pair()
    collect.finish()
    gain_grad[...] = jnp.zeros_like(gain_grad)

    def back(at):
        grad_in[at] = grad_mid[at] + norm_back(
            collect.total(at), hidden[at].astype(F32), gain[...], gain_grad
        )

    row_loop(hidden.shape[0], back)
    moves.close()


class Scatter:
    def __init__(self, moves, place, product, out0, in0, out1, in1, acc, acc_pair, spare):
        self.moves, self.place, self.product, self.spare = moves, place, product, spare
        self.out0, self.in0, self.out1, self.in1, self.acc, self.acc_pair = out0, in0, out1, in1, acc, acc_pair
        self.low, self.high = place.bits[1], place.bits[0]
        self.order = [self.high, self.high | PAIR, 0, PAIR]
        self.first, self.second, self.leaving = {}, {}, {}

    def send(self, i):
        slot = i % 2
        for wait in self.leaving.pop(slot, []):
            wait()

        def emit(at, value):
            self.out0[(slot, *at)] = value.astype(BF16)

        self.product(self.order[i] | self.low, emit)
        self.leaving[slot] = []
        self.first[i] = self.moves.swap(
            self.out0.at[slot], self.in0.at[i], self.in0.at[i], self.place.along(self.low), self.leaving[slot]
        )

    def take(self, i):
        self.first[i]()

        def emit(at, value):
            value = value + self.in0[(i, *at)].astype(F32)
            if i < 2:
                self.out1[(i, *at)] = value.astype(BF16)
            elif i == 2:
                self.acc[at] = value
            else:
                self.acc_pair[at] = value.astype(BF16)

        self.product(self.order[i], emit)
        if i < 2:
            to = self.in1.at[i]
            self.second[i] = Cross(
                self.moves, self.place, self.out1.at[i], to, self.spare.at[2 * i], to, self.spare.at[2 * i + 1], to
            )

    def relay(self, i):
        self.second[i].relay()

    def take_high(self, i):
        self.second[i].arrive()
        total = self.acc_pair if i else self.acc
        step = 64

        @pl.loop(0, total.shape[0] // step)
        def _(k):
            at = pl.ds(pl.multiple_of(k * step, step), step)
            total[at] = (total[at].astype(F32) + self.in1[i, at].astype(F32)).astype(total.dtype)

    def close(self):
        for waits in self.leaving.values():
            for wait in waits:
                wait()


class Blocks:
    def __init__(self, moves, place, slots, order):
        self.moves, self.place, self.slots, self.order = moves, place, slots, order
        self.next, self.waits = 0, {}
        self.start(0)

    def start(self, k):
        if k < len(self.order):
            ref, mask = self.order[k]
            size = self.slots.shape[2]
            at = pl.ds(pl.multiple_of(self.place.block(mask) * size, size), size)
            self.waits[k] = self.moves.load(ref.at[:, at], self.slots.at[k % 2])

    def get(self, ref, mask):
        k = self.next
        assert self.order[k][0] is ref and self.order[k][1] == mask
        self.next += 1
        self.waits.pop(k)()
        self.start(k + 1)
        return self.slots[k % 2]


def backward_kernel(
    bits, groups,
    cot, gain_attn, gain_mlp, starts, cos, sin, gain_q, gain_k,
    mid, hidden, part_two, part_hidden, normed_one, normed_two, cot_rows, qkv_in, att_in, qkv_weight, out_weight, grad_gate, grad_up,
    mixed_t, early_in,
    grad_in, hidden_out, gains, feed_own, feed_other, down_own, down_other, qkv_own, qkv_other, out_own, out_other,
    spare_feed, spare_down, spare_qkv, spare_out,
    own, rows_mid, feed, mixed, lhs, lhs_t, part, w_qkv, w_out, qkv, att, datt, dqkv,
    first, ctx_in, pair_in, sending, first_h, ctx_h, pair_h, sending_h, gain_a, gain_m, gain_h, tree, tree_in,
    f_out0, f_in0, f_out1, f_in1, f_acc, f_pair, d_out0, d_in0, d_out1, d_in1, d_acc, d_pair,
    q_out0, q_in0, q_out1, q_in1, q_acc, q_pair, o_out0, o_in0, o_out1, o_in1, o_acc, o_pair,
    send, recv, local,
):
    place = Place(bits)
    moves = Moves(send, recv, local)
    rows, width = cot.shape
    cols = mixed.shape[0]
    tile = lhs.shape[2]
    half = tile // 2
    high, low = bits
    place.greet()

    def lanes(start, size):
        return pl.ds(pl.multiple_of(start, size), size)

    ready_mid = moves.load(mid, hidden_out)
    ready_feed = [
        moves.load(grad_gate, feed.at[:, pl.ds(0, cols)]),
        moves.load(grad_up, feed.at[:, pl.ds(cols, cols)]),
    ]
    masks = [high, high | PAIR, 0, PAIR]
    sends = [m | low for m in masks]
    a, b, c, e = range(4)
    order = [
        (cot_rows, masks[b]), (cot_rows, sends[e]), (cot_rows, masks[a]), (normed_two, sends[a]),
        (cot_rows, masks[e]), (normed_two, sends[b]), (normed_two, masks[a]), (normed_two, sends[e]),
        (normed_two, masks[b]), (normed_two, masks[e]), (normed_one, sends[a]), (normed_one, sends[b]),
        (normed_one, masks[a]), (normed_two, sends[c]), (normed_one, sends[e]), (normed_one, masks[b]),
        (normed_two, masks[c]), (normed_one, sends[c]), (normed_one, masks[e]), (cot_rows, sends[c]),
        (normed_one, masks[c]), (cot_rows, masks[c]),
    ]
    blocks = Blocks(moves, place, lhs, order)
    ready_mixed = moves.load(mixed_t, mixed)
    ready_early = [moves.load(early_in.at[i], d_in0.at[i]) for i in range(2)]
    ready_late = [
        moves.load(out_weight, w_out),
        moves.load(att_in, att),
        moves.load(qkv_in, qkv),
        moves.load(qkv_weight, w_qkv),
    ]

    def by_rows(source, right):
        def product(mask, emit):
            lhs_t[...] = blocks.get(source, mask).T
            step = min(512, right.shape[1])

            @pl.loop(0, right.shape[1] // step)
            def _(i):
                at = lanes(i * step, step)
                emit((slice(None), at), dot(lhs_t[...], right[:, at]))

        return product

    def down_product(mask, emit):
        block = blocks.get(cot_rows, mask)
        step = min(256, cols)

        @pl.loop(0, cols // step)
        def _(i):
            at = lanes(i * step, step)
            emit((at, slice(None)), dot(mixed[at], block))

    def out_product(mask, emit):
        at = lanes(place.block(mask) * tile, tile)
        emit((slice(None), slice(None)), dot_rows(att[...], rows_mid[:, at]))

    feed_s = Scatter(moves, place, by_rows(normed_two, feed), f_out0, f_in0, f_out1, f_in1, f_acc, f_pair, spare_feed)
    down_s = Scatter(moves, place, down_product, d_out0, d_in0, d_out1, d_in1, d_acc, d_pair, spare_down)
    down_s.first = dict(enumerate(ready_early))
    qkv_s = Scatter(moves, place, by_rows(normed_one, dqkv), q_out0, q_in0, q_out1, q_in1, q_acc, q_pair, spare_qkv)
    out_s = Scatter(moves, place, out_product, o_out0, o_in0, o_out1, o_in1, o_acc, o_pair, spare_out)

    d = gain_q.shape[1]
    gain_m[...] = jnp.zeros_like(gain_m)
    gain_a[...] = jnp.zeros_like(gain_a)
    gain_h[...] = jnp.zeros_like(gain_h)

    twos = [None, None]

    def collect_part(h):
        at = pl.ds(h * rows // 2, rows // 2)
        return Collect(
            moves, place, lambda j, t: part_two.at[place.rows_of[j] + t, at], part.at[:, at], first.at[:, at],
            ctx_in.at[:, at], pair_in.at[at], sending.at[:, at], True,
        )

    def back_two(h):
        def body(there, at):
            x = hidden_out[at]
            g = cot[at].astype(F32) + norm_back(twos[h].total(there), x, gain_mlp[...], gain_m)
            hidden_out[at] = x + collect_hidden.two(0, at)
            grad_in[at] = g
            own[at] = g.astype(BF16)

        return body

    def back_one(at):
        grad_in[at] += norm_back(collect_one.total(at), own[at].astype(F32), gain_attn[...], gain_a)

    def end_hidden(at):
        hidden_out[at] += ctx_h[1, at].astype(F32) + pair_h[at].astype(F32)

    tree_waits = []

    def climb():
        k = len(tree_waits)
        if k == 1:
            tree_waits[0]()
            tree[1] = tree[0] + tree_in[0]
        if k > 1:
            for wait in tree_waits[-1]:
                wait()
            at = 1 + 4 * (k - 2)
            tree[k] = (tree_in[at] + tree_in[at + 1]) + (tree_in[at + 2] + tree_in[at + 3])
        if k == 0:
            tree_waits.append(moves.swap(tree.at[0], tree_in.at[0], tree_in.at[0], place.sibling))
        elif k < 3:
            mine, others = team(k)
            slots = 1 + 4 * (k - 1)
            tree_in[slots + mine] = tree[k]
            tree_waits.append(
                [
                    moves.swap(tree.at[k], tree_in.at[slots + mine], tree_in.at[slots + index], device)
                    for index, device in others
                ]
            )

    def team(k):
        if k == 1:
            return place.rows_of[0] // 2, [(place.rows_of[j] // 2, place.chips[j]) for j in (3, 2, 1)]

        def index(mask):
            f = place.block(mask)
            return (f // high) % 2 * 2 + f % 2

        return index(0), [(index(m), place.along(m)) for m in (high | low, high, low)]

    finals = []

    def pair_final(scatter, other):
        scatter.take_high(1)
        finals.append(moves.swap(scatter.acc_pair, other, other, place.chips[2]))

    def own_final(scatter, mine):
        scatter.take_high(0)
        moves.store(scatter.acc, mine)

    def mates_final(scatter, slot, piece, spare, other):
        scatter.take_high(slot)
        for j in (3, 2) if slot else (1,):
            out = spare(j)
            out[...] = piece(slot, place.at[j][1]).astype(BF16)
            finals.append(moves.swap(out, other.at[j - 1], other.at[j - 1], place.chips[j]))

    def qkv_piece(slot, c):
        return (q_pair if slot else q_acc)[lanes(c * half, half)]

    def out_piece(slot, c):
        return (o_pair if slot else o_acc)[:, lanes(c * half, half)]

    def qkv_spare(j):
        return q_in0.at[j, pl.ds(0, half)]

    def out_spare(j):
        return o_in0.at[j, :, pl.ds(0, half)]

    ready_mixed()
    down_s.take(b)
    twos[0] = collect_part(0)
    down_s.send(e)
    for wait in ready_feed:
        wait()
    twos[0].to_ctx()
    collect_hidden = Collect(
        moves, place, lambda j, t: part_hidden.at[place.rows_of[j] + t], part.at[pl.ds(4, 4)],
        first_h, ctx_h, pair_h, sending_h, True,
    )
    twos[1] = collect_part(1)
    down_s.take(a)
    down_s.relay(b)
    feed_s.send(a)
    collect_hidden.fold()
    down_s.take(e)
    twos[1].to_ctx()
    twos[0].to_pair()
    feed_s.send(b)
    twos[1].to_pair()
    twos[0].finish()
    ready_mid()
    half_loop(0, rows // 2, back_two(0))
    spread_0 = Spread(moves, place, own.at[pl.ds(0 * rows // 2, rows // 2)], rows_mid, 0, 2)
    down_s.relay(a)
    twos[1].finish()
    half_loop(1, rows // 2, back_two(1))
    spread_1 = Spread(moves, place, own.at[pl.ds(1 * rows // 2, rows // 2)], rows_mid, 1, 2)
    feed_s.take(a)
    spread_0.from_pair()
    spread_0.from_ctx()
    for wait in ready_late:
        wait()
    spread_1.from_ctx()
    spread_1.from_pair()
    pair_final(down_s, down_other)
    spread_0.from_both()
    feed_s.send(e)
    spread_1.from_both()
    feed_s.take(b)
    collect_hidden.post_ctx()
    spread_1.finish()
    spread_0.finish()
    ready_hidden = moves.load(hidden, own)
    out_s.send(a)
    @pl.loop(0, 4)
    def _(i):
        at = lanes(i * 2 * rows, 2 * rows)
        datt[at] = dot_cols(rows_mid[at], w_out[...]).astype(BF16)

    out_s.send(b)
    feed_s.relay(a)
    @pl.loop(0, 2)
    def _(s):
        attend_back_one(groups, s, qkv, att, datt, starts, cos, sin, gain_q, gain_k, dqkv, gain_h)

    @pl.loop(0, width // tile)
    def _(i):
        at = lanes(i * tile, tile)
        part[:, :, at] = dot_cols(dqkv[...], w_qkv[at]).astype(BF16).reshape(8, rows, tile)

    feed_s.take(e)
    collect_hidden.post_pair()
    collect_one = Collect(
        moves, place, lambda j, t: part.at[place.rows_of[j] + t], None, first, ctx_in, pair_in, sending, False
    )
    qkv_s.send(a)
    collect_one.to_ctx()
    out_s.send(e)
    out_s.send(c)
    out_s.take(b)
    qkv_s.send(b)
    feed_s.relay(b)
    out_s.take(c)
    qkv_s.take(a)
    feed_s.send(c)
    out_s.relay(b)
    out_s.take(a)
    collect_one.to_pair()
    qkv_s.relay(a)
    qkv_s.send(e)
    collect_hidden.came()
    row_loop(rows, end_hidden)
    out_s.take(e)
    qkv_s.take(b)
    feed_s.take(c)
    own_final(feed_s, feed_own)
    pair_final(feed_s, feed_other)
    collect_one.finish()
    qkv_s.send(c)
    qkv_s.take(e)
    down_s.send(c)
    ready_hidden()
    row_loop(rows, back_one)
    tree[0, :, 0:width] = jnp.sum(gain_a[...], axis=0, keepdims=True)
    tree[0, :, width : 2 * width] = jnp.sum(gain_m[...], axis=0, keepdims=True)
    tree[0, :, 2 * width : 2 * width + d] = jnp.sum(gain_h[0], axis=0, keepdims=True)
    tree[0, :, 2 * width + d : 2 * width + 2 * d] = jnp.sum(gain_h[1], axis=0, keepdims=True)
    climb()
    climb()
    qkv_s.relay(b)
    qkv_s.take(c)
    mates_final(qkv_s, 0, qkv_piece, qkv_spare, qkv_other)
    qkv_own[...] = qkv_piece(0, place.c)
    mates_final(out_s, 1, out_piece, out_spare, out_other)
    climb()
    out_s.relay(a)
    mates_final(qkv_s, 1, qkv_piece, qkv_spare, qkv_other)
    mates_final(out_s, 0, out_piece, out_spare, out_other)
    out_own[...] = out_piece(0, place.c)
    down_s.take(c)
    own_final(down_s, down_own)
    climb()
    gains[...] = tree[3]
    for scatter in (feed_s, down_s, qkv_s, out_s):
        scatter.close()
    for wait in finals:
        wait()
    moves.close()


def join_kernel(
    feed_own, feed_other, down_own, down_other, qkv_own, qkv_other, out_own, out_other, grad_in, hidden, gains,
    g_query, g_key, g_value, g_out, g_gate, g_up, g_down, g_in, h_out, gain_a, gain_m, gain_q, gain_k,
):
    c = lax.axis_index("ctx")
    pair = (lax.axis_index("fsdp") // PAIR) % 2
    cols, n_q = down_own.shape[0], out_own.shape[0]
    n_kv = (qkv_own.shape[1] - n_q) // 2

    def lanes(start, size):
        return pl.ds(pl.multiple_of(start, size), size)

    mine, theirs = lanes(pair * cols, cols), lanes((1 - pair) * cols, cols)
    g_gate[:, mine] = feed_own[:, :cols]
    g_up[:, mine] = feed_own[:, cols:]
    g_down[mine] = down_own[...]
    g_gate[:, theirs] = feed_other[:, :cols].astype(F32)
    g_up[:, theirs] = feed_other[:, cols:].astype(F32)
    g_down[theirs] = down_other[...].astype(F32)
    chunks = [c * 2 + pair, (1 - c) * 2 + pair, c * 2 + 1 - pair, (1 - c) * 2 + 1 - pair]
    for j, chunk in enumerate(chunks):
        qkv = qkv_own[...] if j == 0 else qkv_other[j - 1].astype(F32)
        g_query[:, lanes(chunk * n_q, n_q)] = qkv[:, :n_q]
        g_key[:, lanes(chunk * n_kv, n_kv)] = qkv[:, n_q : n_q + n_kv]
        g_value[:, lanes(chunk * n_kv, n_kv)] = qkv[:, n_q + n_kv :]
        g_out[lanes(chunk * n_q, n_q)] = out_own[...] if j == 0 else out_other[j - 1].astype(F32)
    g_in[...] = grad_in[...]
    h_out[...] = hidden[...]
    width, d = gain_a.shape[1], gain_q.shape[1]
    gain_a[...] = gains[:, :width]
    gain_m[...] = gains[:, width : 2 * width]
    gain_q[...] = gains[:, 2 * width : 2 * width + d]
    gain_k[...] = gains[:, 2 * width + d :]


VMEM_SPEC = pl.BlockSpec(memory_space=pltpu.VMEM)
ANY_SPEC = pl.BlockSpec(memory_space=pl.ANY)


def comm_call(kernel, bits, collective_id, operands, in_specs, outs, out_specs, scratch, nbytes, copies, *more):
    return pl.pallas_call(
        functools.partial(kernel, bits, *more),
        out_shape=outs,
        in_specs=in_specs,
        out_specs=out_specs,
        scratch_shapes=[
            *scratch,
            pltpu.SemaphoreType.DMA((copies,)),
            pltpu.SemaphoreType.DMA((copies,)),
            pltpu.SemaphoreType.DMA((96,)),
        ],
        compiler_params=pltpu.CompilerParams(
            collective_id=collective_id, has_side_effects=True, vmem_limit_bytes=61 << 20
        ),
        cost_estimate=pl.CostEstimate(flops=nbytes * 20, bytes_accessed=nbytes, transcendentals=0),
        name=kernel.__name__,
    )(*operands)


def build(mesh):
    n = mesh.size
    n_f = mesh.shape["fsdp"]
    spread_bits = [b for b in (1 << i for i in range(n_f.bit_length() - 2, -1, -1)) if b != PAIR]
    all_bits = sorted([*spread_bits, PAIR], reverse=True)

    def swap(v, bit):
        return lax.ppermute(v, AXES, [(i, i ^ bit) for i in range(n)])

    def bit_of(f, b):
        return (f // b) % 2

    def in_order(bit, own, other, axis):
        low = jnp.where(bit == 0, own, other)
        high = jnp.where(bit == 0, other, own)
        return jnp.stack([low, high], axis=axis)

    def pick(v, index, axis):
        return lax.dynamic_index_in_dim(v, index, axis, keepdims=False)

    def scatter(keep, got, f, width):
        v = keep + got.astype(F32)
        have = [b for b in all_bits if b != 1]
        v = v.reshape(*([2] * len(have)), width, v.shape[-1])
        for b in [b for b in reversed(spread_bits) if b != 1]:
            axis = have.index(b)
            bit = bit_of(f, b)
            v = pick(v, bit, axis) + swap(pick(v, 1 - bit, axis).astype(BF16), b * 4).astype(F32)
            have.remove(b)
        return v

    def body(
        hidden_in,
        cotangent,
        segments,
        w_query,
        key_projection_weight,
        value_projection_weight,
        w_out,
        w_gate,
        w_up,
        w_down,
        gain_attn,
        gain_mlp,
        gain_query,
        key_norm_gain,
    ):
        rows, width = hidden_in.shape
        d = gain_query.shape[0]
        length = segments.shape[0]
        f, c = lax.axis_index("fsdp"), lax.axis_index("ctx")
        pair = bit_of(f, PAIR)
        at_rows = w_query.shape[0]
        ff_rows = w_gate.shape[0]
        ff_cols = w_gate.shape[1] // 2
        q_cols, kv_cols = w_query.shape[1] // 4, key_projection_weight.shape[1] // 4
        groups = q_cols // kv_cols

        freqs = THETA ** (-2.0 * jnp.arange(d // 2, dtype=F32) / d)
        angles = jnp.arange(length, dtype=jnp.int32).astype(F32)[:, None] * freqs
        table_cos, table_sin = jnp.cos(angles), jnp.sin(angles)
        table = jnp.concatenate([table_cos, table_cos, -table_sin, table_sin], axis=-1)

        n_rows = 8 * rows
        all_rows = jax.ShapeDtypeStruct((n_rows, width), BF16)
        own_rows = jax.ShapeDtypeStruct((rows, width), F32)
        gain_rows = jax.ShapeDtypeStruct((8, width), F32)
        block = pltpu.VMEM((rows, width), BF16)
        nbytes = rows * width * 16
        qkv_cols = q_cols + 2 * kv_cols

        def shape(*dims):
            return jax.ShapeDtypeStruct(dims, BF16)

        copies = 160 + 10 * n_f
        natural = at_rows % 128 == 0 and ff_rows % 128 == 0
        out_dims = (q_cols, width) if natural else (width, q_cols)
        down_dims = (ff_cols, width) if natural else (width, ff_cols)
        out_part = (q_cols, 2 * at_rows) if natural else (2 * at_rows, q_cols)
        down_part_dims = (ff_cols, ff_rows) if natural else (ff_rows, ff_cols)
        border = ff_cols - 256 if ff_cols % 256 == 0 and ff_cols > 256 else ff_cols // 2
        feed_spares = []
        for piece in (border, ff_cols - border):
            feed_spares += [shape(4, ff_rows, piece)] * 2
            feed_spares.append(shape(4, piece, ff_rows) if natural else shape(4, ff_rows, piece))
        n_seq = 2 * length
        all_tables = jax.ShapeDtypeStruct((n_seq, d), F32)

        def v(*dims, dtype=BF16):
            return pltpu.VMEM(dims, dtype)

        (
            residual_mid, normed_one, normed_two, grad_rows, qkv, attended, full_qkv, full_out, starts, cos, sin,
            grad_gate, grad_up, mixed_t, norm_two_part, down_part, *_, early_in,
        ) = comm_call(
            forward_kernel, spread_bits, 0,
            (hidden_in, cotangent, gain_attn[None], gain_mlp[None], segments[None], table, gain_query[None],
             key_norm_gain[None], w_query, key_projection_weight, value_projection_weight,
             w_out if natural else w_out.T, w_gate, w_up, w_down if natural else w_down.T),
            [VMEM_SPEC] * 8 + [ANY_SPEC] * 7,
            (own_rows, all_rows, all_rows, all_rows, shape(n_rows, qkv_cols), shape(n_rows, q_cols),
             shape(width, qkv_cols), shape(*out_dims), jax.ShapeDtypeStruct((n_seq, 128), F32), all_tables, all_tables,
             shape(n_rows, ff_cols), shape(n_rows, ff_cols), shape(ff_cols, n_rows), shape(8, rows, width), all_rows,
             shape(4, 2 * at_rows, qkv_cols), shape(4, *out_part), *feed_spares,
             shape(2, *down_part_dims)),
            (VMEM_SPEC, *[ANY_SPEC] * 24),
            [block, block, v(n_rows, width), v(n_rows, width), v(n_rows, width), v(width, qkv_cols), v(*out_dims),
             v(width, ff_cols), v(width, ff_cols), v(*down_dims), v(n_rows, qkv_cols), v(n_rows, q_cols),
             v(8, rows, width), v(n_rows, ff_cols, dtype=F32), v(n_rows, ff_cols, dtype=F32), v(n_rows, ff_cols),
             v(n_rows, ff_cols), v(n_rows, ff_cols), v(ff_cols, n_rows), v(n_seq, 128, dtype=F32),
             v(n_seq, d, dtype=F32), v(n_seq, d, dtype=F32), v(1, length, dtype=jnp.int32), v(2, *down_part_dims),
             *collect_buffers(rows, width)],
            16 * nbytes, copies, groups, natural,
        )
        common = (starts, cos, sin, gain_query[None], key_norm_gain[None])
        backward = one_kernel if natural and len(spread_bits) == 2 else by_steps
        return backward(
            hidden_in, cotangent, residual_mid, gain_attn, gain_mlp, common, norm_two_part, down_part, normed_one,
            normed_two, grad_rows, qkv, attended, full_qkv, full_out, grad_gate, grad_up, mixed_t, early_in,
            (at_rows, ff_rows),
        )

    def one_kernel(
        hidden_in, cotangent, residual_mid, gain_attn, gain_mlp, common, norm_two_part, down_part, normed_one,
        normed_two, grad_rows, qkv, attended, full_qkv, full_out, grad_gate, grad_up, mixed_t, early_in, sizes,
    ):
        rows, width = hidden_in.shape
        cols, n_rows = mixed_t.shape
        (at_rows, ff_rows), q_cols, qkv_cols = sizes, attended.shape[1], qkv.shape[1]
        d = common[-1].shape[1]
        kv_cols = (qkv_cols - q_cols) // 2
        groups = q_cols // kv_cols

        def out(dtype, *dims):
            return jax.ShapeDtypeStruct(dims, dtype)

        def v(*dims, dtype=BF16):
            return pltpu.VMEM(dims, dtype)

        def scatter(*block):
            return [v(2, *block), v(4, *block), v(2, *block), v(2, *block), v(*block, dtype=F32), v(*block)]

        n_gain = 2 * width + 2 * d
        nbytes = n_rows * width * 20
        (
            grad_input, hidden_out, gains, feed_own, feed_other, down_own, down_other, qkv_own, qkv_other, out_own,
            out_other, *_,
        ) = comm_call(
            backward_kernel, spread_bits, 2,
            (cotangent, gain_attn[None], gain_mlp[None], *common, residual_mid, hidden_in, norm_two_part,
             down_part.reshape(8, rows, width), normed_one, normed_two, grad_rows, qkv, attended, full_qkv, full_out,
             grad_gate, grad_up, mixed_t, early_in),
            [VMEM_SPEC] * 8 + [ANY_SPEC] * 15,
            (out(F32, rows, width), out(F32, rows, width), out(F32, 1, n_gain), out(F32, ff_rows, 2 * cols),
             out(BF16, ff_rows, 2 * cols), out(F32, cols, ff_rows), out(BF16, cols, ff_rows),
             out(F32, at_rows, qkv_cols), out(BF16, 3, at_rows, qkv_cols), out(F32, q_cols, at_rows),
             out(BF16, 3, q_cols, at_rows), out(BF16, 4, ff_rows, 2 * cols), out(BF16, 4, cols, ff_rows),
             out(BF16, 4, ff_rows, qkv_cols), out(BF16, 4, q_cols, ff_rows)),
            (VMEM_SPEC, VMEM_SPEC, VMEM_SPEC, ANY_SPEC, ANY_SPEC, ANY_SPEC, ANY_SPEC, VMEM_SPEC, ANY_SPEC, VMEM_SPEC,
             *[ANY_SPEC] * 5),
            [v(rows, width), v(n_rows, width), v(n_rows, 2 * cols), v(cols, n_rows), v(2, n_rows, ff_rows),
             v(ff_rows, n_rows), v(8, rows, width), v(width, qkv_cols), v(q_cols, width), v(n_rows, qkv_cols),
             v(n_rows, q_cols), v(n_rows, q_cols), v(n_rows, qkv_cols),
             *collect_buffers(rows, width), *collect_buffers(rows, width), v(8, width, dtype=F32), v(8, width, dtype=F32), v(2, 8, d, dtype=F32),
             v(4, 1, n_gain, dtype=F32), v(9, 1, n_gain, dtype=F32),
             *scatter(ff_rows, 2 * cols), *scatter(cols, ff_rows), *scatter(ff_rows, qkv_cols),
             *scatter(q_cols, ff_rows)],
            nbytes, 110, groups,
        )
        own_rows = out(F32, rows, width)
        made = (
            out(F32, at_rows, 4 * q_cols), out(F32, at_rows, 4 * kv_cols), out(F32, at_rows, 4 * kv_cols),
            out(F32, 4 * q_cols, at_rows), out(F32, ff_rows, 2 * cols), out(F32, ff_rows, 2 * cols),
            out(F32, 2 * cols, ff_rows), own_rows, own_rows, out(F32, 1, width), out(F32, 1, width), out(F32, 1, d),
            out(F32, 1, d),
        )
        pieces = pl.pallas_call(
            join_kernel,
            out_shape=made,
            compiler_params=pltpu.CompilerParams(vmem_limit_bytes=61 << 20),
            name="join_kernel",
        )(feed_own, feed_other, down_own, down_other, qkv_own, qkv_other, out_own, out_other, grad_input, hidden_out, gains)
        grads, (grad_input, hidden_out), gains = pieces[:7], pieces[7:9], pieces[9:]
        return hidden_out, grad_input, *grads, *(g[0] for g in gains)

    def by_steps(
        hidden_in, cotangent, residual_mid, gain_attn, gain_mlp, common, norm_two_part, down_part, normed_one,
        normed_two, grad_rows, qkv, attended, full_qkv, full_out, grad_gate, grad_up, mixed_t, early_in, sizes,
    ):
        rows, width = hidden_in.shape
        (at_rows, ff_rows), ff_cols, q_cols = sizes, mixed_t.shape[0], attended.shape[1]
        d = common[-1].shape[1]
        kv_cols = (qkv.shape[1] - q_cols) // 2
        groups = q_cols // kv_cols
        natural = full_out.shape[0] != width
        times_t = dot_cols if natural else dot
        f, c = lax.axis_index("fsdp"), lax.axis_index("ctx")
        pair = bit_of(f, PAIR)
        all_rows = jax.ShapeDtypeStruct((8 * rows, width), BF16)
        own_rows = jax.ShapeDtypeStruct((rows, width), F32)
        gain_rows = jax.ShapeDtypeStruct((8, width), F32)
        block = pltpu.VMEM((rows, width), BF16)
        nbytes = rows * width * 16
        grad_mid, gain_mlp_part, grad_mid_rows = comm_call(
            turn_kernel, spread_bits, 2, (norm_two_part.reshape(8, rows, width), residual_mid, cotangent, gain_mlp[None]),
            [ANY_SPEC, VMEM_SPEC, VMEM_SPEC, VMEM_SPEC], (own_rows, gain_rows, all_rows),
            (VMEM_SPEC, VMEM_SPEC, ANY_SPEC),
            [block, pltpu.VMEM((4, rows, width), BF16), *collect_buffers(rows, width)], 2 * nbytes, 40,
        )

        low = bit_of(f, 1)

        def weight_grad(acts, grads):
            split = acts.reshape(acts.shape[0], n_f // 2, 2, width // n_f)
            mine = pick(split, low, 2).reshape(acts.shape[0], -1)
            theirs = pick(split, 1 - low, 2).reshape(acts.shape[0], -1)
            got = swap(dot_rows(theirs, grads).astype(BF16), 4)
            return scatter(dot_rows(mine, grads), got, f, width // n_f)

        def ff_grad(acts, grads):
            v = weight_grad(acts, grads)
            other = swap(pick(v, 1 - pair, 0).astype(BF16), PAIR_BIT).astype(F32)
            return in_order(pair, pick(v, pair, 0), other, 1).reshape(ff_rows, 2 * ff_cols)

        grad_w_gate = ff_grad(normed_two, grad_gate)
        grad_w_up = ff_grad(normed_two, grad_up)
        grad_w_down = ff_grad(grad_rows, mixed_t.T).T

        def attn_grad(acts, grads):
            v = weight_grad(acts, grads)
            v = v.reshape(2, 2, at_rows, v.shape[-1])
            mine = pick(pick(v, pair, 0), c, 0)
            by_ctx = swap(pick(pick(v, pair, 0), 1 - c, 0).astype(BF16), CTX_BIT).astype(F32)
            by_pair = swap(pick(pick(v, 1 - pair, 0), c, 0).astype(BF16), PAIR_BIT).astype(F32)
            by_both = swap(pick(pick(v, 1 - pair, 0), 1 - c, 0).astype(BF16), CTX_BIT | PAIR_BIT).astype(F32)
            near = in_order(pair, mine, by_pair, 1)
            far = in_order(pair, by_ctx, by_both, 1)
            return in_order(c, near, far, 1)

        grad_w_out = attn_grad(grad_mid_rows, attended).reshape(at_rows, 4 * q_cols).T

        datt = times_t(grad_mid_rows, full_out).astype(BF16)
        grad_qkv, head_gains = attend_back(groups, qkv, attended, datt, common)
        norm_one_part = dot_cols(grad_qkv, full_qkv).astype(BF16)
        grad_input, gain_attn_part = comm_call(
            last_kernel, spread_bits, 3, (norm_one_part.reshape(8, rows, width), hidden_in, grad_mid, gain_attn[None]),
            [ANY_SPEC, VMEM_SPEC, VMEM_SPEC, VMEM_SPEC], (own_rows, gain_rows), (VMEM_SPEC, VMEM_SPEC),
            [pltpu.VMEM((4, rows, width), BF16), *collect_buffers(rows, width)], nbytes, 40,
        )
        grad_qkv_w = attn_grad(normed_one, grad_qkv)
        grad_w_query = grad_qkv_w[..., :q_cols].reshape(at_rows, -1)
        grad_w_key = grad_qkv_w[..., q_cols : q_cols + kv_cols].reshape(at_rows, -1)
        grad_w_value = grad_qkv_w[..., q_cols + kv_cols :].reshape(at_rows, -1)

        head_gains = jnp.sum(head_gains, axis=1)
        gains = jnp.concatenate(
            [jnp.sum(gain_attn_part, axis=0), jnp.sum(gain_mlp_part, axis=0), head_gains[0], head_gains[1]]
        ).reshape(-1, d)
        for i in range(n.bit_length() - 1):
            gains = gains + swap(gains, 1 << i)
        gains = gains.reshape(-1)
        teams = sorted(
            sorted(i ^ b ^ p for b in range(4) for p in (0, PAIR_BIT))
            for i in range(0, n, 4)
            if not i & PAIR_BIT
        )
        hidden_out = residual_mid + lax.psum_scatter(
            down_part, AXES, scatter_dimension=0, axis_index_groups=teams, tiled=True
        ).astype(F32)
        return (
            hidden_out,
            grad_input,
            grad_w_query,
            grad_w_key,
            grad_w_value,
            grad_w_out,
            grad_w_gate,
            grad_w_up,
            grad_w_down,
            gains[:width],
            gains[width : 2 * width],
            gains[2 * width : 2 * width + d],
            gains[2 * width + d :],
        )

    return body


def solution(mesh):
    everyone = P(("fsdp", "ctx", "tp"), None)
    attn = P(("fsdp", "ctx"), "tp")
    attn_out = P("tp", ("fsdp", "ctx"))
    ff_in = P("fsdp", ("ctx", "tp"))
    ff_out = P(("ctx", "tp"), "fsdp")
    same = P()
    return jax.shard_map(
        build(mesh),
        mesh=mesh,
        in_specs=(
            everyone, everyone, P("fsdp"), attn, attn, attn, attn_out, ff_in, ff_in, ff_out,
            same, same, same, same,
        ),
        out_specs=(
            everyone, everyone, attn, attn, attn, attn_out, ff_in, ff_in, ff_out,
            same, same, same, same,
        ),
        check_vma=False,
    )
```

profile of v0, /device:TPU:0, one launch (start us, length us, event | category | flops | bytes accessed | tf_op | source)
XLA Modules:
  0.0 375.1 jit_solution(5368512839459508827)
XLA Ops:
  0.7 1.0 multiply_cosine_fusion
  1.7 1.1 pad_maximum_fusion.table
  2.7 194.1 %forward_kernel.1 = (f32[128,2048]{1,0:T(8,128)}, bf16[1024,2048]{1,0:T(8,128)(2,1)}, bf16[1024,2048]{1,0:T(8,128)(2,1)}, bf16[1024,2048]{1,0:T(8,128)(2,1)}, bf...) custom-call(bf16[128,2048]{1,0:T(8,128)(2,1)} %hidden.3, ...), custom_call_target="tpu_custom_call" | custom-call | flops 1342177280 | bytes 67108864 | tf_op jit(solution)/shard_map/forward_kernel/pallas_call | solution.py:1332
  196.9 171.4 %backward_kernel.1 = (f32[128,2048]{1,0:T(8,128)}, f32[128,2048]{1,0:T(8,128)}, f32[1,4352]{1,0:T(1,128)}, f32[256,1536]{1,0:T(8,128)}, bf16[256,1536]{1,0:T(8,1...) custom-call(bf16[128,2048]{1,0:T(8,128)(2,1)} %cot.3, ...), custom_call_target="tpu_custom_call" | custom-call | flops 838860800 | bytes 41943040 | tf_op jit(solution)/shard_map/backward_kernel/pallas_call | solution.py:1332
  368.3 6.6 %join_kernel.1 = (f32[128,1024]{1,0:T(8,128)}, f32[128,512]{1,0:T(8,128)}, f32[128,512]{1,0:T(8,128)}, f32[1024,128]{1,0:T(8,128)}, f32[256,1536]{1,0:T(8,128)},...) custom-call(f32[256,1536]{1,0:T(8,128)} %get-tuple-element.71.feed_o, ...), custom_call_target="tpu_custom_call" | custom-call | tf_op jit(solution)/shard_map/join_kernel/pallas_call | solution.py:1527
  (2 shorter events, 0.0 us)
where the time goes:
time: 375 us
  Pallas kernels  372 us (99%)
    pallas_call x2, Pallas kernels, comm_call(): pl.pallas_call(functools.partial(kernel, bits, *more), out_shape=outs, in...  366 us

commit v1 on v0

--- a/solution.py
+++ b/solution.py
@@ -105,8 +105,8 @@
 
 
 class Cross:
-    def __init__(self, moves, place, src, here, came_in, across_to, came_out, pair_to):
-        self.place, self.here = place, here
+    def __init__(self, moves, place, src, here, came_in, across_to, came_out, pair_to, held=None):
+        self.place, self.here, self.held = place, here, held
         self.came_in, self.came_out = came_in, came_out
         k = moves.sent
         moves.sent += 4
@@ -117,7 +117,7 @@
 
         self.hand = copy(0, src, came_in, pair)
         self.own = copy(1, src, came_out, across)
-        self.on = copy(2, came_in, across_to, across)
+        self.on = copy(2, came_in if held is None else held, across_to, across)
         self.back = copy(3, came_out, pair_to, pair)
         self.came = [copy(0, came_in, came_in, pair), copy(1, came_out, came_out, across)]
         self.landed = [copy(2, here, here, across), copy(3, here, here, pair)]
@@ -126,16 +126,20 @@
         @pl.when(place.inner)
         def _():
             self.own.start()
+            if held is not None:
+                self.on.start()
 
         @pl.when(jnp.logical_not(place.inner))
         def _():
-            self.hand.start()
+            if held is None:
+                self.hand.start()
 
     def relay(self):
         @pl.when(self.place.inner)
         def _():
-            self.came[0].wait_recv()
-            self.on.start()
+            if self.held is None:
+                self.came[0].wait_recv()
+                self.on.start()
             self.came[1].wait_recv()
             self.back.start()
 
@@ -157,7 +161,8 @@
 
         @pl.when(jnp.logical_not(self.place.inner))
         def _():
-            self.hand.wait_send()
+            if self.held is None:
+                self.hand.wait_send()
 
 
 class Spread:
@@ -328,7 +333,7 @@
         self.moves, self.place, self.block, self.spare = moves, place, block, spare
         self.waits, self.crosses = {}, {}
 
-    def forward(self, mask, src=None):
+    def forward(self, mask, src=None, held=None):
         done = [i for i, b in enumerate(self.place.bits) if mask & b]
         here = self.block(self.place.block(mask))
         for b in self.place.bits[max(done, default=-1) + 1 :]:
@@ -338,7 +343,7 @@
                 self.crosses[mask] = Cross(
                     self.moves, self.place, here if src is None else src, self.block(self.place.block(mask | b)),
                     self.spare.at[slot], self.block(self.place.block(mask ^ PAIR)),
-                    self.spare.at[slot + 1], self.block(self.place.block(mask ^ far)),
+                    self.spare.at[slot + 1], self.block(self.place.block(mask ^ far)), held,
                 )
                 self.waits[mask | b] = self.crosses[mask].arrive
                 continue
@@ -362,9 +367,9 @@
         elif m == PAIR:
             self.middle()
 
-    def pass_on(self, m):
+    def pass_on(self, m, held=None):
         self.waits.pop(m)()
-        self.forward(m)
+        self.forward(m, None, held)
 
     def middle(self):
         for stage in range(len(self.place.bits) - 1):
@@ -660,6 +665,7 @@
         fj, cj, _ = place.at[j]
         out_in[j] = moves.swap(out_chunk(j), out_block(f0, c0), out_block(fj, cj), place.chips[j])
     out_in[0] = moves.load(out_chunk(0), out_block(f0, c0))
+    feed[1][0].forward(0, feed[1][1])
     for j in (1, 3, 2):
         fj, cj, _ = place.at[j]
         qkv_in[j] = [
@@ -675,39 +681,38 @@
         moves.load(w.at[:, lanes(place.chunk_of[0] * size, size)], w_qkv.at[qkv_rows(f0, c0), to])
         for w, size, to in pieces
     ]
-    out_in[0]()
-    out_in[1]()
-    out_gather.forward(0)
+    row_loop(rows, norm_one)
+    spread_one = Spread(moves, place, own_one, rows_one)
     for wait in (*qkv_in[0], *qkv_in[1]):
         wait()
     qkv_gather.forward(0)
+    feed[1][0].relay(0)
     for wait in (*qkv_in[2], *qkv_in[3]):
         wait()
     qkv_gather.forward(PAIR)
     out_in[2]()
     out_in[3]()
     out_gather.forward(PAIR)
-    row_loop(rows, norm_one)
-    spread_one = Spread(moves, place, own_one, rows_one)
+    out_in[0]()
+    out_in[1]()
+    out_gather.forward(0)
+    feed[0][0].forward(0, feed[0][1])
+    seg_wait = moves.swap(seg, seg_in, seg_in, place.chips[2])
+    swap_pair(0)
+    spread_one.from_pair()
+    swap_pair(1)
+    qkv_gather.relay(0)
+    qkv_gather.relay(PAIR)
+    qkv_gather.hop(0)
+    spread_one.from_both()
     out_gather.relay(0)
-    seg_wait = moves.swap(seg, seg_in, seg_in, place.chips[2])
-    qkv_gather.relay(0)
-    swap_pair(1)
-    qkv_gather.relay(PAIR)
-    feed[2][0].forward(0, feed[2][1])
-    swap_pair(2)
-    qkv_gather.hop(0)
     out_gather.relay(PAIR)
-    feed[3][0].forward(0, feed[3][1])
+    qkv_gather.hop(PAIR)
+    feed[0][0].relay(0)
+    spread_cot = Spread(moves, place, cot, rows_cot)
+    swap_pair(5)
     out_gather.hop(0)
-    spread_one.from_pair()
-    qkv_gather.hop(PAIR)
-    feed[0][0].forward(0, feed[0][1])
-    spread_cot = Spread(moves, place, cot, rows_cot)
-    spread_one.from_both()
-    out_gather.hop(PAIR)
     spread_one.from_ctx()
-    feed[1][0].forward(0, feed[1][1])
     seg_wait()
     pair_first = place.pair == 0
     own_seg, far_seg = seg[...].astype(F32), seg_in[...].astype(F32)
@@ -731,16 +736,13 @@
     moves.store(starts, starts_out)
     moves.store(cos, cos_out)
     moves.store(sin, sin_out)
-    feed[2][0].pass_on(PAIR)
     spread_one.finish()
     normed_stored = moves.load(rows_one, normed_one)
-    feed[2][0].relay(0)
-    feed[1][0].pass_on(PAIR)
-    swap_pair(0)
+    out_gather.hop(PAIR)
+    feed[0][0].pass_on(PAIR, feed[0][2])
+    feed[3][0].forward(0, feed[3][1])
     qkv_gather.finish()
     moves.store(w_qkv, qkv_weight)
-    swap_pair(3)
-    feed[0][0].relay(0)
     @pl.loop(0, w_qkv.shape[1] // wide)
     def _(i):
         at = lanes(i * wide, wide)
@@ -752,98 +754,101 @@
         attend_one(groups, s, qkv, starts, cos, sin, gain_q, gain_k, att)
 
     moves.store(att, att_out)
-    swap_pair(4)
+    feed[1][0].pass_on(PAIR, feed[1][2])
     out_gather.finish()
     moves.store(w_out, out_weight)
-    feed[2][0].hop(0)
-    feed[4][0].forward(0, feed[4][1])
+    feed[1][0].hop(0)
+    feed[0][0].relay(PAIR)
     @pl.loop(0, width // 256)
     def _(i):
         at = lanes(i * 256, 256)
         times, block = columns_of(w_out, at)
         part[:, :, at] = times(att[...], block).astype(BF16).reshape(8, rows, 256)
 
+    swap_pair(4)
     collects[0] = collect_part(0)
-    feed[1][0].relay(0)
+    collects[1] = collect_part(1)
     collects[0].to_ctx()
-    collects[1] = collect_part(1)
+    swap_pair(2)
+    feed[4][0].forward(0, feed[4][1])
+    collects[1].to_ctx()
+    swap_pair(3)
+    collects[0].to_pair()
+    feed[2][0].forward(0, feed[2][1])
+    feed[4][0].pass_on(PAIR, feed[4][2])
+    feed[1][0].relay(PAIR)
+    feed[0][0].hop(0)
+    collects[1].to_pair()
+    feed[4][0].relay(0)
+    collects[0].finish()
+    feed[4][0].relay(PAIR)
     feed[3][0].relay(0)
-    feed[1][0].relay(PAIR)
-    feed[1][0].hop(0)
-    collects[1].to_ctx()
-    feed[2][0].relay(PAIR)
-    feed[0][0].pass_on(PAIR)
+    half_loop(0, rows // 2, norm_two(0))
+    feed[2][0].pass_on(PAIR, feed[2][2])
+    spread_two_0 = Spread(moves, place, own_two.at[pl.ds(0 * rows // 2, rows // 2)], rows_two, 0, 2)
+    feed[1][0].hop(PAIR)
+    feed[3][0].pass_on(PAIR, feed[3][2])
     spread_cot.from_pair()
-    collects[1].to_pair()
-    spread_cot.from_ctx()
-    collects[0].to_pair()
-    feed[3][0].pass_on(PAIR)
-    feed[2][0].hop(PAIR)
-    feed[0][0].relay(PAIR)
-    feed[3][0].hop(0)
-    feed[0][0].hop(0)
     collects[1].finish()
     half_loop(1, rows // 2, norm_two(1))
+    feed[5][0].forward(0, feed[5][1])
     spread_two_1 = Spread(moves, place, own_two.at[pl.ds(1 * rows // 2, rows // 2)], rows_two, 1, 2)
-    feed[1][0].hop(PAIR)
+    feed[0][0].hop(PAIR)
+    feed[4][0].hop(0)
+    feed[2][0].relay(0)
+    feed[3][0].relay(PAIR)
+    spread_cot.from_ctx()
+    spread_cot.from_both()
+    feed[3][0].hop(0)
+    spread_two_0.from_ctx()
+    spread_two_0.from_pair()
+    spread_cot.finish()
+    moves.store(rows_cot, cot_out)
+    feed[2][0].relay(PAIR)
+    spread_two_1.from_ctx()
+    feed[5][0].pass_on(PAIR, feed[5][2])
+    feed[4][0].hop(PAIR)
+    feed[5][0].relay(0)
+    own_feed[0]()
+    feed[0][0].finish()
+    spread_two_1.from_pair()
+    spread_two_0.from_both()
+    feed[2][0].hop(0)
+    spread_two_1.from_both()
+    own_feed[4]()
+    feed[4][0].finish()
+    spread_two_0.finish()
+    own_feed[1]()
+    feed[1][0].finish()
+    feed[5][0].relay(PAIR)
+    feed[3][0].hop(PAIR)
+    spread_two_1.finish()
+    moves.store(rows_two, normed_two)
+    gate_part(piece_a)
+    feed[2][0].hop(PAIR)
+    up_part(piece_a)
+    own_feed[3]()
+    feed[3][0].finish()
+    feed[5][0].hop(0)
+    gate_part(piece_b)
+    up_part(piece_b)
+    send_early(0)
+    moves.store(mixed_t, mixed_out)
+    feed[5][0].hop(PAIR)
     own_feed[2]()
     feed[2][0].finish()
-    collects[0].finish()
-    half_loop(0, rows // 2, norm_two(0))
-    spread_two_0 = Spread(moves, place, own_two.at[pl.ds(0 * rows // 2, rows // 2)], rows_two, 0, 2)
-    feed[0][0].hop(PAIR)
-    spread_cot.from_both()
-    feed[4][0].pass_on(PAIR)
-    feed[3][0].relay(PAIR)
-    spread_two_1.from_pair()
-    swap_pair(5)
-    feed[4][0].relay(0)
-    spread_cot.finish()
-    moves.store(rows_cot, cot_out)
-    own_feed[0]()
-    feed[0][0].finish()
-    spread_two_0.from_pair()
-    feed[3][0].hop(PAIR)
-    spread_two_0.from_ctx()
-    spread_two_1.from_ctx()
-    feed[5][0].forward(0, feed[5][1])
-    feed[4][0].relay(PAIR)
-    spread_two_1.from_both()
-    own_feed[3]()
-    feed[3][0].finish()
-    own_feed[1]()
-    feed[1][0].finish()
-    feed[4][0].hop(0)
-    feed[5][0].pass_on(PAIR)
-    spread_two_0.from_both()
-    spread_two_1.finish()
-    feed[4][0].hop(PAIR)
-    feed[5][0].relay(0)
-    spread_two_0.finish()
-    moves.store(rows_two, normed_two)
-    gate_part(piece_a)
-    feed[5][0].relay(PAIR)
-    gate_part(piece_b)
-    up_part(piece_a)
-    feed[5][0].hop(0)
-    own_feed[4]()
-    feed[4][0].finish()
-    feed[5][0].hop(PAIR)
-    up_part(piece_b)
-    send_early(0)
-    send_early(1)
     normed_stored()
     down_part(piece_a, False)
+    back_part(piece_a)
+    send_early(1)
+    grad_part(piece_a, False)
     own_feed[5]()
     feed[5][0].finish()
-    back_part(piece_a)
     back_part(piece_b)
-    down_part(piece_b, True)
-    grad_part(piece_a, False)
-    grad_part(piece_b, True)
-    moves.store(mixed_t, mixed_out)
     moves.store(grad_gate, grad_gate_out)
     moves.store(grad_up, grad_up_out)
+    grad_part(piece_b, True)
+    down_part(piece_b, True)
     for wait in early_waits:
         wait()
     moves.close()

time: 375 us -> 367 us (0.979)
  Pallas kernels: 372 us -> 364 us
    pallas_call x2, Pallas kernels: 366 us -> 358 us  [comm_call(): pl.pallas_call(functools.partial(kernel, bits, *more), out_shape=outs, in...]
where the time goes in v1:
time: 367 us
  Pallas kernels  364 us (99%)
    pallas_call x2, Pallas kernels, comm_call(): pl.pallas_call(functools.partial(kernel, bits, *more), out_shape=outs, in...  358 us

profile of v1, /device:TPU:0, one launch (start us, length us, event | category | flops | bytes accessed | tf_op | source)
XLA Modules:
  0.0 367.1 jit_solution(3092428185933483593)
XLA Ops:
  0.7 1.0 multiply_cosine_fusion
  1.7 1.1 pad_maximum_fusion.table
  2.7 187.6 %forward_kernel.1 = (f32[128,2048]{1,0:T(8,128)}, bf16[1024,2048]{1,0:T(8,128)(2,1)}, bf16[1024,2048]{1,0:T(8,128)(2,1)}, bf16[1024,2048]{1,0:T(8,128)(2,1)}, bf...) custom-call(bf16[128,2048]{1,0:T(8,128)(2,1)} %hidden.3, ...), custom_call_target="tpu_custom_call" | custom-call | flops 1342177280 | bytes 67108864 | tf_op jit(solution)/shard_map/forward_kernel/pallas_call | solution.py:1337
  190.4 169.9 %backward_kernel.1 = (f32[128,2048]{1,0:T(8,128)}, f32[128,2048]{1,0:T(8,128)}, f32[1,4352]{1,0:T(1,128)}, f32[256,1536]{1,0:T(8,128)}, bf16[256,1536]{1,0:T(8,1...) custom-call(bf16[128,2048]{1,0:T(8,128)(2,1)} %cot.3, ...), custom_call_target="tpu_custom_call" | custom-call | flops 838860800 | bytes 41943040 | tf_op jit(solution)/shard_map/backward_kernel/pallas_call | solution.py:1337
  360.3 6.6 %join_kernel.1 = (f32[128,1024]{1,0:T(8,128)}, f32[128,512]{1,0:T(8,128)}, f32[128,512]{1,0:T(8,128)}, f32[1024,128]{1,0:T(8,128)}, f32[256,1536]{1,0:T(8,128)},...) custom-call(f32[256,1536]{1,0:T(8,128)} %get-tuple-element.71.feed_o, ...), custom_call_target="tpu_custom_call" | custom-call | tf_op jit(solution)/shard_map/join_kernel/pallas_call | solution.py:1532
  (2 shorter events, 0.0 us)

commit v2 on v1

--- a/solution.py
+++ b/solution.py
@@ -2,6 +2,7 @@
 
 import jax
 import jax.numpy as jnp
+import numpy as np
 from jax import lax
 from jax.experimental import pallas as pl
 from jax.experimental.pallas import tpu as pltpu
@@ -1411,10 +1412,10 @@
         q_cols, kv_cols = w_query.shape[1] // 4, key_projection_weight.shape[1] // 4
         groups = q_cols // kv_cols
 
-        freqs = THETA ** (-2.0 * jnp.arange(d // 2, dtype=F32) / d)
-        angles = jnp.arange(length, dtype=jnp.int32).astype(F32)[:, None] * freqs
-        table_cos, table_sin = jnp.cos(angles), jnp.sin(angles)
-        table = jnp.concatenate([table_cos, table_cos, -table_sin, table_sin], axis=-1)
+        freqs = (THETA ** (-2.0 * np.arange(d // 2, dtype=np.float32) / d)).astype(np.float32)
+        angles = (np.arange(length, dtype=np.float32)[:, None] * freqs).astype(np.float64)
+        table_cos, table_sin = np.cos(angles), np.sin(angles)
+        table = jnp.asarray(np.concatenate([table_cos, table_cos, -table_sin, table_sin], axis=-1), F32)
 
         n_rows = 8 * rows
         all_rows = jax.ShapeDtypeStruct((n_rows, width), BF16)

time: 367 us -> 366 us (level)
  no operation moved by 1% of the time
where the time goes in v2:
time: 366 us; the launch traced here: 365 us
  Pallas kernels  364 us (99%)
    pallas_call x2, Pallas kernels, comm_call(): pl.pallas_call(functools.partial(kernel, bits, *more), out_shape=outs, in...  358 us

profile of v2, /device:TPU:0, one launch (start us, length us, event | category | flops | bytes accessed | tf_op | source)
XLA Modules:
  0.0 365.1 jit_solution(642222450235725033)
XLA Ops:
  0.6 187.7 %forward_kernel.1 = (f32[128,2048]{1,0:T(8,128)}, bf16[1024,2048]{1,0:T(8,128)(2,1)}, bf16[1024,2048]{1,0:T(8,128)(2,1)}, bf16[1024,2048]{1,0:T(8,128)(2,1)}, bf...) custom-call(bf16[128,2048]{1,0:T(8,128)(2,1)} %hidden.3, ...), custom_call_target="tpu_custom_call" | custom-call | flops 1342177280 | bytes 67108864 | tf_op jit(solution)/shard_map/forward_kernel/pallas_call | solution.py:1338
  188.4 169.9 %backward_kernel.1 = (f32[128,2048]{1,0:T(8,128)}, f32[128,2048]{1,0:T(8,128)}, f32[1,4352]{1,0:T(1,128)}, f32[256,1536]{1,0:T(8,128)}, bf16[256,1536]{1,0:T(8,1...) custom-call(bf16[128,2048]{1,0:T(8,128)(2,1)} %cot.3, ...), custom_call_target="tpu_custom_call" | custom-call | flops 838860800 | bytes 41943040 | tf_op jit(solution)/shard_map/backward_kernel/pallas_call | solution.py:1338
  358.3 6.6 %join_kernel.1 = (f32[128,1024]{1,0:T(8,128)}, f32[128,512]{1,0:T(8,128)}, f32[128,512]{1,0:T(8,128)}, f32[1024,128]{1,0:T(8,128)}, f32[256,1536]{1,0:T(8,128)},...) custom-call(f32[256,1536]{1,0:T(8,128)} %get-tuple-element.71.feed_o, ...), custom_call_target="tpu_custom_call" | custom-call | tf_op jit(solution)/shard_map/join_kernel/pallas_call | solution.py:1533
